TPU v7x, 512 devices: a whole 4x8x8 slice. The times are simulated.
512 devices in a mesh: mod: 2 (over z_hi), loop: 16 (over x, z_lo), line: 16 (over y, core).
Axes of the slice: x: 4, y: 8, z: 8 (z_hi: 2, z_lo: 4; z = z_hi * 4 + z_lo), core: 2. Of those that a mesh axis runs over, the one named last changes fastest.
Arguments:
- act: bfloat16 [2, 196608, 512], P('mod', ('loop', 'line'))
- dy: bfloat16 [2, 196608, 1280], P('mod', ('loop', 'line')), may hold values from -6 to 6
- w_out: bfloat16 [2, 512, 1280], P('mod'), may hold values from -0.15625 to 0.15625
- counts: int32 [2, 16, 16], P('mod', 'loop', 'line'), may hold values from 192 to 768, as said below
Outputs:
- grad_clipped: float32 [2, 512, 1280], P('mod', 'loop')
- hidden_grad: bfloat16 [2, 196608, 512], P('mod', ('loop', 'line'))
Inputs may be any that keep to these rules, and one draw needn't show every extreme that they name: `counts`: in each tower some device has all 768 slots live.
All inputs are finite; a program needn't handle non-finite values.
Results may differ from a plain program's by a relative error of at most 0.001.
Values sent between devices are 32-bit elements; how exact they have to be, the bound alone decides.
A program may use at most 64 MiB of HBM per device.

v0:
```python
import jax
import jax.numpy as jnp
from jax import lax
from jax.sharding import PartitionSpec as P


def on_device(act, dy, w_out, counts):
    tokens = act[0]
    upstream = dy[0]
    weight = w_out[0]
    rows = tokens.shape[0]
    hidden = tokens.shape[1]
    block = weight.shape[1]
    live = lax.broadcasted_iota(jnp.int32, (rows, 1), 0) < counts[0, 0]
    masked = jnp.where(live, tokens, jnp.zeros_like(tokens))
    entries = lax.axis_size("mod") * hidden * block
    share = lax.psum_scatter(
        lax.dot_general(
            masked, upstream, (((0,), (0,)), ((), ())), preferred_element_type=jnp.float32
        ),
        "loop",
        scatter_dimension=0,
        tiled=True,
    )
    share = lax.psum(share, "line")
    total = lax.psum(jnp.sum(share * share), ("mod", "loop"))
    factor = 1.0 / jnp.sqrt(total / entries + 1e-06)
    clipped = share * factor
    back = lax.dot_general(
        upstream, weight, (((1,), (1,)), ((), ())), preferred_element_type=jnp.float32
    )
    hidden_grad = jnp.where(live, back, jnp.zeros_like(back)).astype(jnp.bfloat16)
    return (clipped[None], hidden_grad[None])


def solution(mesh):
    in_specs = (
        P("mod", ("loop", "line"), None),
        P("mod", ("loop", "line"), None),
        P("mod", None, None),
        P("mod", "loop", "line"),
    )
    out_specs = (P("mod", "loop", None), P("mod", ("loop", "line"), None))
    return jax.shard_map(
        on_device, mesh=mesh, in_specs=in_specs, out_specs=out_specs, check_vma=False
    )
```

profile of v0, /device:TPU:8, one launch (start us, length us, event | category | flops | bytes accessed | tf_op | source)
XLA Modules:
  0.0 310.6 jit_solution(13326542029925265666)
XLA Ops:
  7.2 0.0 copy-start
  7.2 0.0 reduce-scatter.2.cloned.1.call-start
  8.0 0.7 copy-done
  8.7 3.9 %fusion.2 = f32[512,1280]{1,0:T(8,128)} fusion(bf16[1,768,1280]{2,1,0:T(8,128)(2,1)S(1)} %copy-done, bf16[1,768,512]{2,1,0:T(8,128)(2,1)} %param.4, pred[768]{0:T(1024)(128)(4,1)S(1)} %iota_compare_fusion), kind=kOutput, calls=%fused_computation.2 | convolution fusion | flops 1007026176 | bytes 5374720 | tf_op jit(solution)/shard_map/dot_general | solution.py:18
  12.7 0.0 copy-start.2
  12.7 0.0 reduce-scatter.2.cloned.1.call-update
  12.7 0.0 all-reduce.2.cloned.1.call-start
  12.8 101.7 %reduce-scatter.2.cloned.1.call-done = f32[32,1280]{1,0:T(8,128)} async-done(((f32[512,1280]{1,0:T(8,128)}), f32[32,1280]{1,0:T(8,128)}) %reduce-scatter.2.cloned.1.call-update) | async-done | bytes 163856 | tf_op jit(solution)/shard_map/reduce_scatter | solution.py:17
  114.5 0.0 all-reduce.2.cloned.1.call-update
  114.5 108.3 %all-reduce.2.cloned.1.call-done = f32[32,1280]{1,0:T(8,128)} async-done(((f32[32,1280]{1,0:T(8,128)}), f32[32,1280]{1,0:T(8,128)}) %all-reduce.2.cloned.1.call-update) | async-done | bytes 163856 | tf_op jit(solution)/shard_map/psum | solution.py:25
  222.8 1.6 multiply_reduce_fusion
  224.4 0.0 copy-done.2
  224.4 0.0 copy-start.1
  224.4 2.1 fusion.7
  226.5 75.9 %psum.15 = f32[]{:T(128)} all-reduce(f32[]{:T(128)} %multiply_reduce_fusion), channel_id=1, replica_groups=mesh['mod'=2,'loop'=16,'line'=16] {'mod','loop'}, use_global_device_ids=true, to_apply=%region_3.4 | all-reduce | flops 1 | bytes 8 | tf_op jit(solution)/shard_map/psum | solution.py:26
  303.1 0.0 copy-done.1
  303.1 0.7 multiply_bitcast_fusion
  (1 shorter events, 0.0 us)
Async XLA Ops:
  7.2 1.6 copy-start
  7.2 107.3 %reduce-scatter.2.cloned.1.call-start = ((), (), s32[]{:S(2)}) async-start(), calls=%async_computation.1 | async-start | bytes 2785280 | tf_op jit(solution)/shard_map/reduce_scatter | solution.py:17
  12.7 211.7 %copy-start.2 = (bf16[1,512,1280]{2,1,0:T(8,128)(2,1)S(1)}, bf16[1,512,1280]{2,1,0:T(8,128)(2,1)}, u32[]{:S(2)}) copy-start(bf16[1,512,1280]{2,1,0:T(8,128)(2,1)} %param.6) | copy-start | bytes 3932164
  12.7 210.1 %all-reduce.2.cloned.1.call-start = ((), (), s32[]{:S(2)}) async-start(), calls=%async_computation.2 | async-start | bytes 327680 | tf_op jit(solution)/shard_map/psum | solution.py:25
  224.4 78.7 %copy-start.1 = (f32[32,1280]{1,0:T(8,128)S(1)}, f32[32,1280]{1,0:T(8,128)}, u32[]{:S(2)}) copy-start(f32[32,1280]{1,0:T(8,128)} %all-reduce.2.cloned.1.call-done) | copy-start | bytes 491524
Sparse Core Ops, SparseCore 0:
  12.8 101.6 reduce-scatter.1
  116.8 105.9 all-reduce.1
where the time goes:
time: 311 us
  waiting for transfers between devices  210 us (68%)
  blocking collectives  75.9 us (24%)
  between operations  15.5 us (5%)
  matrix products  6.04 us (2%)
    psum x1, waiting for transfers between devices, on_device(): share = lax.psum(share, 'line')  108 us
    reduce_scatter x1, waiting for transfers between devices, on_device(): lax.psum_scatter(lax.dot_general(masked, upstream, (((0,), (0,)), ((), ()...  102 us
    psum x1, blocking collectives, on_device(): total = lax.psum(jnp.sum(share * share), ('mod', 'loop'))  75.9 us
  transfers between devices with their start and end apart: 2, of which 2 were waited for; matrix products, arithmetic and copies ran while one was open for 0% of the time, Pallas kernels for 0%

commit v1 on v0

--- a/solution.py
+++ b/solution.py
@@ -22,7 +22,12 @@
         scatter_dimension=0,
         tiled=True,
     )
-    share = lax.psum(share, "line")
+
+    def remake_sums_all_now(array_in):
+        part_next = lax.all_gather(array_in, axis_name="line")
+        return jnp.sum(part_next, 0)
+
+    share = remake_sums_all_now(share)
     total = lax.psum(jnp.sum(share * share), ("mod", "loop"))
     factor = 1.0 / jnp.sqrt(total / entries + 1e-06)
     clipped = share * factor

time: 311 us -> 246 us (0.79)
  waiting for transfers between devices: 210 us -> 143 us
    psum x1 -> x0, waiting for transfers between devices: 108 us -> none  [on_device(): share = lax.psum(share, 'line')]
    all_gather x0 -> x1, waiting for transfers between devices: none -> 41.7 us  [remake_sums_all_now(): part_next = lax.all_gather(array_in, axis_name='line')]
where the time goes in v1:
time: 246 us; the launch traced here: 245 us
  waiting for transfers between devices  143 us (58%)
  blocking collectives  76.3 us (31%)
  between operations  15.5 us (6%)
  matrix products  6.04 us (2%)
  other arithmetic  3.2 us (1%)
    reduce_scatter x1, waiting for transfers between devices, on_device(): lax.psum_scatter(lax.dot_general(masked, upstream, (((0,), (0,)), ((), ()...  102 us
    psum x1, blocking collectives, on_device(): total = lax.psum(jnp.sum(share * share), ('mod', 'loop'))  76.3 us
    all_gather x1, waiting for transfers between devices, remake_sums_all_now(): part_next = lax.all_gather(array_in, axis_name='line')  41.7 us
  transfers between devices with their start and end apart: 2, of which 2 were waited for; matrix products, arithmetic and copies ran while one was open for 0% of the time, Pallas kernels for 0%

profile of v1, /device:TPU:8, one launch (start us, length us, event | category | flops | bytes accessed | tf_op | source)
XLA Modules:
  0.0 245.4 jit_solution(3424943287230502218)
XLA Ops:
  7.2 0.0 copy-start
  7.2 0.0 reduce-scatter.2.cloned.1.call-start
  8.0 0.7 copy-done
  8.7 3.9 %fusion.2 = f32[512,1280]{1,0:T(8,128)} fusion(bf16[1,768,1280]{2,1,0:T(8,128)(2,1)S(1)} %copy-done, bf16[1,768,512]{2,1,0:T(8,128)(2,1)} %param.4, pred[768]{0:T(1024)(128)(4,1)S(1)} %iota_compare_fusion), kind=kOutput, calls=%fused_computation.2 | convolution fusion | flops 1007026176 | bytes 5374720 | tf_op jit(solution)/shard_map/dot_general | solution.py:18
  12.7 0.0 reduce-scatter.2.cloned.1.call-update
  12.7 0.0 copy-start.1
  12.7 0.0 all-gather.3.cloned.1.call-start
  12.8 101.7 %reduce-scatter.2.cloned.1.call-done = f32[32,1280]{1,0:T(8,128)} async-done(((f32[512,1280]{1,0:T(8,128)}), f32[32,1280]{1,0:T(8,128)}) %reduce-scatter.2.cloned.1.call-update) | async-done | bytes 163856 | tf_op jit(solution)/shard_map/reduce_scatter | solution.py:17
  114.5 0.0 all-gather.3.cloned.1.call-update
  114.5 41.7 %all-gather.3.cloned.1.call-done = f32[512,1280]{1,0:T(8,128)} async-done(((f32[32,1280]{1,0:T(8,128)}), f32[512,1280]{1,0:T(8,128)}) %all-gather.3.cloned.1.call-update) | async-done | bytes 2621456 | tf_op jit(solution)/shard_map/all_gather | solution.py:27
  156.3 1.9 reduce_sum.18
  158.1 0.6 multiply_reduce_fusion
  158.8 0.0 copy-done.1
  158.8 2.1 fusion.7
  160.9 76.3 %psum.7 = f32[]{:T(128)} all-reduce(f32[]{:T(128)} %multiply_reduce_fusion), channel_id=1, replica_groups=mesh['mod'=2,'loop'=16,'line'=16] {'mod','loop'}, use_global_device_ids=true, to_apply=%region_3.4 | all-reduce | flops 1 | bytes 8 | tf_op jit(solution)/shard_map/psum | solution.py:31
  237.8 0.7 multiply_bitcast_fusion
  (1 shorter events, 0.0 us)
Async XLA Ops:
  7.2 1.6 copy-start
  7.2 107.3 %reduce-scatter.2.cloned.1.call-start = ((), (), s32[]{:S(2)}) async-start(), calls=%async_computation.1 | async-start | bytes 2785280 | tf_op jit(solution)/shard_map/reduce_scatter | solution.py:17
  12.7 146.1 %copy-start.1 = (bf16[1,512,1280]{2,1,0:T(8,128)(2,1)S(1)}, bf16[1,512,1280]{2,1,0:T(8,128)(2,1)}, u32[]{:S(2)}) copy-start(bf16[1,512,1280]{2,1,0:T(8,128)(2,1)} %param.6) | copy-start | bytes 3932164
  12.7 143.5 %all-gather.3.cloned.1.call-start = ((), (), s32[]{:S(2)}) async-start(), calls=%async_computation.2 | async-start | bytes 2785280 | tf_op jit(solution)/shard_map/all_gather | solution.py:27
Sparse Core Ops, SparseCore 0:
  12.8 101.6 reduce-scatter.1
  116.6 39.5 all-gather.2
